TPU v7x, 32 devices: a whole 2x2x4 slice. The times are simulated.
32 devices in a mesh: groups: 2 (over y), ctx: 4 (over x, core), head: 4 (over z).
Axes of the slice: x: 2, y: 2, z: 4, core: 2. Of those that a mesh axis runs over, the one named last changes fastest.
Arguments:
- context: bfloat16 [8192, 1024], P(('groups', 'ctx', 'head')), parts along dimension 0, may hold values from -6 to 6
- w_kv: bfloat16 [1024, 2048], replicated, may hold values from -0.1875 to 0.1875
- queries: bfloat16 [32, 64, 2048], P(('groups', 'head')), parts along dimension 0, may hold values from -400 to 400
- gain: float32 [1024], replicated, may hold values from 0.25 to 1.75
- w_out: bfloat16 [1024, 1024], P('head'), may hold values from -0.1875 to 0.1875
Outputs:
- latent_out: bfloat16 [4096, 1024], P(('groups', 'ctx', 'head')), parts along dimension 0
There are 2 independent parts, one for each index of `groups`. A program takes and returns all parts, laid end to end along the dimension named above; an argument that names none is the same for every part. Nothing has to cross between parts.
All inputs are finite; a program needn't handle non-finite values.
Results may differ from a plain program's by a relative error of at most 0.01575.
Values may be sent and summed in bfloat16 or wider, within the bound.
No kernel may reach another device: no remote copies, remote signals or barrier semaphores. Data moves between devices by JAX's collectives and lax.ppermute only.
A program may use at most 64 MiB of HBM per device.

v0:
```python
import math
import jax
import jax.numpy as jnp
from jax import lax
from jax.sharding import PartitionSpec as P

epsilon = 1e-06


def body(context, w_kv, queries, gain, w_out):
    heads_local, head_size, latents = queries.shape
    model_width = w_kv.shape[0]
    total_heads = w_kv.shape[1] // (2 * head_size)
    head_count = lax.axis_size("head")
    ctx_count = lax.axis_size("ctx")
    head_scale = 1.0 / math.sqrt(head_size)
    projected = jnp.dot(context, w_kv, preferred_element_type=jnp.float32).astype(jnp.bfloat16)
    projected = projected.reshape(context.shape[0], total_heads, 2 * head_size)
    regrouped = lax.all_to_all(projected, "head", split_axis=1, concat_axis=0, tiled=True)
    key_rows = regrouped[:, :, :head_size]
    value_rows = regrouped[:, :, head_size:]
    block_size = min(512, latents)
    block_count = latents // block_size
    query_blocks = queries.reshape(heads_local, head_size, block_count, block_size)

    def attend(position):
        query_block = lax.dynamic_index_in_dim(query_blocks, position, 2, keepdims=False)
        scores = (
            jnp.einsum("hdq,khd->hqk", query_block, key_rows, preferred_element_type=jnp.float32)
            * head_scale
        )
        highest = jnp.max(scores, axis=2)
        weights = jnp.exp(scores - highest[:, :, None])
        row_total = jnp.sum(weights, axis=2)
        summed = jnp.einsum(
            "hqk,khd->hqd",
            weights.astype(jnp.bfloat16),
            value_rows,
            preferred_element_type=jnp.float32,
        )
        return (highest, row_total, summed)

    maxima, totals, partials = lax.map(attend, jnp.arange(block_count))
    maxima = maxima.transpose(1, 0, 2).reshape(heads_local, latents)
    totals = totals.transpose(1, 0, 2).reshape(heads_local, latents)
    partials = partials.transpose(1, 0, 2, 3).reshape(heads_local, latents * head_size // 128, 128)
    ctx_rows = latents // ctx_count
    overall = lax.pmax(maxima, "ctx")
    factor = jnp.exp(maxima - overall)
    spread = partials.reshape(heads_local, latents, head_size) * factor[:, :, None]
    scaled = spread.reshape(heads_local, latents * head_size // 128, 128)
    sums_own, total_own = (
        lax.psum_scatter(
            scaled.astype(jnp.bfloat16), "ctx", scatter_dimension=1, tiled=True
        ).astype(jnp.float32),
        lax.psum_scatter(
            (totals * factor).astype(jnp.bfloat16), "ctx", scatter_dimension=1, tiled=True
        ).astype(jnp.float32),
    )
    sums_own = sums_own.reshape(heads_local, ctx_rows, head_size)
    attended = sums_own / total_own[:, :, None]
    own_rows = ctx_rows // head_count
    packed = attended.reshape(heads_local, head_count, own_rows * head_size)
    gathered = lax.all_to_all(
        packed.astype(jnp.bfloat16), "head", split_axis=1, concat_axis=0, tiled=True
    ).astype(packed.dtype)
    joined = (
        gathered.reshape(total_heads, own_rows, head_size)
        .transpose(1, 0, 2)
        .reshape(own_rows, model_width)
    )
    mean_square = jnp.sum(joined * joined, axis=1, keepdims=True) / model_width
    normed = (joined * gain[None, :] * lax.rsqrt(mean_square + epsilon)).astype(jnp.bfloat16)
    result = jnp.dot(
        normed,
        lax.all_gather(w_out, "head", axis=0, tiled=True),
        preferred_element_type=jnp.float32,
    )
    return result.astype(jnp.bfloat16)


def solution(mesh):
    return jax.shard_map(
        body,
        mesh=mesh,
        in_specs=(
            P(("groups", "ctx", "head"), None),
            P(),
            P(("groups", "head"), None, None),
            P(),
            P("head", None),
        ),
        out_specs=P(("groups", "ctx", "head"), None),
        check_vma=False,
    )
```

profile of v0, /device:TPU:0, one launch (start us, length us, event | category | flops | bytes accessed | tf_op | source)
XLA Modules:
  0.0 184.5 jit_solution(581980694861545381)
XLA Ops:
  8.4 3.4 %fusion.15 = bf16[32,16,8,128]{3,2,1,0:T(8,128)(2,1)S(1)} fusion(bf16[256,1024]{1,0:T(8,128)(2,1)S(1)} %copy-done, bf16[1024,2048]{1,0:T(8,128)(2,1)} %param.8), kind=kOutput, calls=%fused_computation.16 | convolution fusion | flops 1074266112 | bytes 5767168 | tf_op jit(solution)/shard_map/dot_general | solution.py:17
  11.9 1.3 copy.24
  13.1 6.3 %all-to-all-start = ((bf16[256,16,128]{2,0,1:T(8,128)(2,1)}), bf16[256,16,128]{2,0,1:T(8,128)(2,1)S(1)}, u32[]{:S(2)}, u32[]{:S(2)}) async-start(bf16[256,16,128]{2,0,1:T(8,128)(2,1)} %bitcast.58), calls=%async_computation | async-start | bytes 2097152 | tf_op jit(solution)/shard_map/all_to_all | solution.py:19
  19.5 1.3 copy.25
  20.8 24.4 %all-to-all-done = bf16[256,16,128]{2,0,1:T(8,128)(2,1)S(1)} async-done(((bf16[256,16,128]{2,0,1:T(8,128)(2,1)}), bf16[256,16,128]{2,0,1:T(8,128)(2,1)S(1)}, u32[]{:S(2)}, u32[]{:S(2)}) %all-to-all-start) | async-done | bytes 1048608 | tf_op jit(solution)/shard_map/all_to_all | solution.py:19
  45.2 1.5 copy.13
  46.7 2.6 %all_to_all.23 = bf16[1024,4,128]{0,2,1:T(8,128)(2,1)} reshape(bf16[4,256,4,128]{1,0,3,2:T(4,128)(2,1)} %copy.13) | data formatting | bytes 2097152 | tf_op jit(solution)/shard_map/all_to_all | solution.py:19
  49.2 1.3 fusion.18
  50.5 32.3 %while.14 = (s32[]{:T(128)}, f32[4,4,512]{2,1,0:T(4,128)S(1)}, f32[4,4,512]{2,1,0:T(4,128)S(1)}, f32[4,4,512,64]{2,3,1,0:T(8,128)}, s32[4]{0:T(128)S(1)}, /*inde...) while((s32[]{:T(128)}, f32[4,4,512]{2,1,0:T(4,128)S(1)}, ...), condition=%wide.region_3.4_spmd, body=%wide.region_0.3_spmd.sunk | while | flops 553644032 | bytes 27067044 | solution.py:43
  52.8 1.4 multiply_reduce_fusion.3
  54.2 2.6 %fusion.34 = f32[4,4,512,64]{2,3,1,0:T(8,128)} fusion(f32[4,4,512,64]{2,3,1,0:T(8,128)} %get-tuple-element.163, s32[]{:T(128)} %get-tuple-element.160, bf16[1024,4,64]{0,2,1:T(8,128)(2,1)S(1)} %get-tuple-element.178, f32[4,512,1024]{2,1,0:T(8,128)S(1)} %get-tuple-element.145, f32[4,512]{1,0:T(4,128)S(1)} %get-tuple-element.146), kind=kOutput, calls=%fused_computation.6.clone.1 | convolution fusion | flops 274726912 | bytes 9445888 | tf_op jit(solution)/shard_map/while/body/eval_jaxpr/hqk,khd->hqd/dot_general | solution.py:35
  56.8 1.8 fusion.33
  60.9 1.4 multiply_reduce_fusion.3
  62.3 2.6 %fusion.34 = f32[4,4,512,64]{2,3,1,0:T(8,128)} fusion(f32[4,4,512,64]{2,3,1,0:T(8,128)} %get-tuple-element.163, s32[]{:T(128)} %get-tuple-element.160, bf16[1024,4,64]{0,2,1:T(8,128)(2,1)S(1)} %get-tuple-element.178, f32[4,512,1024]{2,1,0:T(8,128)S(1)} %get-tuple-element.145, f32[4,512]{1,0:T(4,128)S(1)} %get-tuple-element.146), kind=kOutput, calls=%fused_computation.6.clone.1 | convolution fusion | flops 274726912 | bytes 9445888 | tf_op jit(solution)/shard_map/while/body/eval_jaxpr/hqk,khd->hqd/dot_general | solution.py:35
  64.9 1.8 fusion.33
  69.0 1.4 multiply_reduce_fusion.3
  70.4 2.6 %fusion.34 = f32[4,4,512,64]{2,3,1,0:T(8,128)} fusion(f32[4,4,512,64]{2,3,1,0:T(8,128)} %get-tuple-element.163, s32[]{:T(128)} %get-tuple-element.160, bf16[1024,4,64]{0,2,1:T(8,128)(2,1)S(1)} %get-tuple-element.178, f32[4,512,1024]{2,1,0:T(8,128)S(1)} %get-tuple-element.145, f32[4,512]{1,0:T(4,128)S(1)} %get-tuple-element.146), kind=kOutput, calls=%fused_computation.6.clone.1 | convolution fusion | flops 274726912 | bytes 9445888 | tf_op jit(solution)/shard_map/while/body/eval_jaxpr/hqk,khd->hqd/dot_general | solution.py:35
  72.9 1.8 fusion.33
  77.0 1.4 multiply_reduce_fusion.3
  78.4 2.6 %fusion.34 = f32[4,4,512,64]{2,3,1,0:T(8,128)} fusion(f32[4,4,512,64]{2,3,1,0:T(8,128)} %get-tuple-element.163, s32[]{:T(128)} %get-tuple-element.160, bf16[1024,4,64]{0,2,1:T(8,128)(2,1)S(1)} %get-tuple-element.178, f32[4,512,1024]{2,1,0:T(8,128)S(1)} %get-tuple-element.145, f32[4,512]{1,0:T(4,128)S(1)} %get-tuple-element.146), kind=kOutput, calls=%fused_computation.6.clone.1 | convolution fusion | flops 274726912 | bytes 9445888 | tf_op jit(solution)/shard_map/while/body/eval_jaxpr/hqk,khd->hqd/dot_general | solution.py:35
  81.0 1.8 fusion.33
  82.8 10.4 %pmax.7 = f32[4,2048]{1,0:T(4,128)S(1)} all-reduce(f32[4,2048]{1,0:T(4,128)S(1)} %bitcast.79), channel_id=1, replica_groups=mesh['groups'=2,'ctx'=4,'head'=4] {'ctx'}, use_global_device_ids=true, to_apply=%region_4.5 | all-reduce | flops 8192 | bytes 65536 | tf_op jit(solution)/shard_map/pmax | solution.py:48
  93.2 2.6 %mul.37 = f32[4,2048,64]{2,1,0:T(8,128)} broadcast(f32[4,2048]{1,0:T(4,128)S(1)} %get-tuple-element.85), dimensions={0,1} | broadcast | bytes 2129920 | tf_op jit(solution)/shard_map/mul | solution.py:50
  95.8 4.6 %mul.38 = f32[4,1024,128]{2,1,0:T(8,128)} reshape(f32[4,2048,64]{2,1,0:T(8,128)} %mul.37) | data formatting | bytes 4194304 | tf_op jit(solution)/shard_map/mul | solution.py:50
  100.5 3.8 %copy.15 = f32[4,4,512,64]{3,2,1,0:T(8,128)} copy(f32[4,4,512,64]{2,3,0,1:T(8,128)} %bitcast.75) | data formatting | bytes 4194304 | tf_op jit(solution)/shard_map/transpose | solution.py:46
  104.2 4.6 %reshape_reshape.3 = f32[4,1024,128]{2,1,0:T(8,128)} reshape(f32[4,4,512,64]{3,2,1,0:T(8,128)} %copy.15) | data formatting | bytes 4194304 | tf_op jit(solution)/shard_map/reshape;reshape | solution.py:50
  110.0 3.4 %multiply_convert_fusion = bf16[4,1024,128]{2,1,0:T(8,128)(2,1)} fusion(f32[4,1024,128]{2,1,0:T(8,128)} %reshape_reshape.3, f32[4,1024,128]{2,1,0:T(8,128)} %mul.38), kind=kLoop, calls=%fused_computation.15 | loop fusion | flops 1048576 | bytes 5242880 | tf_op jit(solution)/shard_map/convert_element_type | solution.py:54
  114.0 16.9 %reduce-scatter.7.cloned.1.call-done = bf16[512,4]{1,0:T(8,128)(2,1)} async-done(((bf16[2048,4]{1,0:T(8,128)(2,1)}), bf16[512,4]{1,0:T(8,128)(2,1)}) %reduce-scatter.7.cloned.1.call-update) | async-done | bytes 4112
  132.7 25.6 %reduce-scatter.5.cloned.1.call-done = bf16[4,256,128]{2,1,0:T(8,128)(2,1)} async-done(((bf16[4,1024,128]{2,1,0:T(8,128)(2,1)}), bf16[4,256,128]{2,1,0:T(8,128)(2,1)}) %reduce-scatter.5.cloned.1.call-update) | async-done | bytes 262160 | tf_op jit(solution)/shard_map/reduce_scatter | solution.py:53
  158.3 1.2 reshape.56
  159.8 13.1 %all_to_all.27 = bf16[4,4,8192]{2,0,1:T(4,128)(2,1)S(1)} all-to-all(bf16[4,4,8192]{2,0,1:T(4,128)(2,1)S(1)} %copy.16), channel_id=1, replica_groups=mesh['groups'=2,'ctx'=4,'head'=4] {'head'}, dimensions={1} | all-to-all | bytes 524288 | tf_op jit(solution)/shard_map/all_to_all | solution.py:64
  174.3 2.8 %convolution_convert_fusion.1 = bf16[128,1024]{1,0:T(8,128)(2,1)} fusion(bf16[128,1024]{0,1:T(8,128)(2,1)S(1)} %fusion.17, bf16[1024,1024]{1,0:T(8,128)(2,1)} %all-gather.2.cloned.1.call-done), kind=kOutput, calls=%fused_computation.17 | convolution fusion | flops 268566528 | bytes 2621440 | tf_op jit(solution)/shard_map/dot_general | solution.py:74
  (36 shorter events, 8.6 us)
Async XLA Ops:
  7.4 1.0 copy-start
  13.1 32.1 %all-to-all-start = ((bf16[256,16,128]{2,0,1:T(8,128)(2,1)}), bf16[256,16,128]{2,0,1:T(8,128)(2,1)S(1)}, u32[]{:S(2)}, u32[]{:S(2)}) async-start(bf16[256,16,128]{2,0,1:T(8,128)(2,1)} %bitcast.58), calls=%async_computation | async-start | bytes 2097152 | tf_op jit(solution)/shard_map/all_to_all | solution.py:19
  19.5 111.4 %reduce-scatter.7.cloned.1.call-start = ((), (), s32[]{:S(2)}) async-start(), calls=%async_computation.6 | async-start | bytes 655360
  109.9 48.3 %reduce-scatter.5.cloned.1.call-start = ((), (), s32[]{:S(2)}) async-start(), calls=%async_computation.4 | async-start | bytes 1310720 | tf_op jit(solution)/shard_map/reduce_scatter | solution.py:53
  113.5 60.8 %all-gather.2.cloned.1.call-start = ((), (), s32[]{:S(2)}) async-start(), calls=%async_computation.5 | async-start | bytes 2621440 | tf_op jit(solution)/shard_map/all_gather | solution.py:76
  132.7 41.3 %copy-start.1 = (f32[1024]{0:T(1024)S(1)}, f32[1024]{0:T(1024)}, u32[]{:S(2)}) copy-start(f32[1024]{0:T(1024)} %param.10) | copy-start | bytes 12292
Sparse Core Ops, SparseCore 0:
  110.1 20.8 reduce-scatter.6
  133.4 24.7 reduce-scatter.4
Sparse Core Ops, SparseCore 1:
  115.5 44.6 all-gather.1
where the time goes:
time: 185 us; the launch traced here: 184 us
  waiting for transfers between devices  67.4 us (36%)
  local copies, waits for them, and re-layouts  32 us (17%)
  blocking collectives  23.5 us (13%)
  matrix products  22.1 us (12%)
  between operations  15 us (8%)
  other arithmetic  11.3 us (6%)
  loops' own time  6.81 us (4%)
  starting transfers between devices  6.43 us (3%)
    reduce_scatter x1, waiting for transfers between devices, body(): lax.psum_scatter(scaled.astype(jnp.bfloat16), 'ctx', scatter_dimension=1,...  25.6 us
    all_to_all x1, waiting for transfers between devices, body(): lax.all_to_all(projected, 'head', split_axis=1, concat_axis=0, tiled=True)  24.4 us
    unnamed x4, waiting for transfers between devices  17.4 us
    all_to_all x1, blocking collectives, body(): lax.all_to_all(packed.astype(jnp.bfloat16), 'head', split_axis=1, concat_...  13.1 us
    pmax x1, blocking collectives, body(): overall = lax.pmax(maxima, 'ctx')  10.4 us
    dot_general x4, matrix products, attend(): jnp.einsum('hqk,khd->hqd', weights.astype(jnp.bfloat16), value_rows, pref...  10.3 us
    reduce_sum x4, other arithmetic, attend(): row_total = jnp.sum(weights, axis=2)  7.21 us
    mul x2, local copies, waits for them, and re-layouts, body(): partials.reshape(heads_local, latents, head_size) * factor[:, :, None]  7.21 us
  transfers between devices with their start and end apart: 4, of which 3 were waited for; matrix products, arithmetic and copies ran while one was open for 5% of the time, Pallas kernels for 0%

commit v1 on v0

--- a/solution.py
+++ b/solution.py
@@ -16,7 +16,18 @@
     head_scale = 1.0 / math.sqrt(head_size)
     projected = jnp.dot(context, w_kv, preferred_element_type=jnp.float32).astype(jnp.bfloat16)
     projected = projected.reshape(context.shape[0], total_heads, 2 * head_size)
-    regrouped = lax.all_to_all(projected, "head", split_axis=1, concat_axis=0, tiled=True)
+    ways, here = (lax.axis_size("head"), lax.axis_index("head"))
+    width = projected.shape[1] // ways
+    shape = list(projected.shape)
+    shape[1] = width
+    height = shape[0]
+    shape[0] = height * ways
+    regrouped = jnp.zeros(shape, projected.dtype)
+    for mask in range(ways):
+        part = lax.dynamic_slice_in_dim(projected, (here ^ mask) * width, width, axis=1)
+        if mask:
+            part = lax.ppermute(part, "head", [(d, d ^ mask) for d in range(ways)])
+        regrouped = lax.dynamic_update_slice_in_dim(regrouped, part, (here ^ mask) * height, axis=0)
     key_rows = regrouped[:, :, :head_size]
     value_rows = regrouped[:, :, head_size:]
     block_size = min(512, latents)

time: 185 us -> 180 us (0.973)
  waiting for transfers between devices: 67.4 us -> 64 us
    all_to_all x1 -> x0, waiting for transfers between devices: 24.4 us -> none  [body(): lax.all_to_all(projected, 'head', split_axis=1, concat_axis=0, tiled=True)]
    ppermute x0 -> x3, waiting for transfers between devices: none -> 16.6 us  [body(): part = lax.ppermute(part, 'head', [(d, d ^ mask) for d in range(ways)])]
    all_to_all x1 -> x0, starting transfers between devices: 6.35 us -> none  [body(): lax.all_to_all(projected, 'head', split_axis=1, concat_axis=0, tiled=True)]
    ppermute x0 -> x3, starting transfers between devices: none -> 5.63 us  [body(): part = lax.ppermute(part, 'head', [(d, d ^ mask) for d in range(ways)])]
    unnamed x4, waiting for transfers between devices: 17.4 us -> 21.8 us
    all_to_all x2 -> x0, local copies, waits for them, and re-layouts: 4.04 us -> none  [body(): lax.all_to_all(projected, 'head', split_axis=1, concat_axis=0, tiled=True)]
    dynamic_update_slice x0 -> x3, local copies, waits for them, and re-layouts: none -> 2.22 us  [body(): lax.dynamic_update_slice_in_dim(regrouped, part, (here ^ mask) * height,...]
  transfers between devices with their start and end apart: 4 -> 6, of which waited for: 3 -> 4; matrix products, arithmetic and copies ran while one was open for 5% -> 6% of each run, Pallas kernels for 0% -> 0%
where the time goes in v1:
time: 180 us; the launch traced here: 179 us
  waiting for transfers between devices  64 us (36%)
  local copies, waits for them, and re-layouts  30.2 us (17%)
  blocking collectives  23.4 us (13%)
  matrix products  22.2 us (12%)
  between operations  15 us (8%)
  other arithmetic  10.6 us (6%)
  loops' own time  7.68 us (4%)
  starting transfers between devices  5.72 us (3%)
    reduce_scatter x1, waiting for transfers between devices, body(): lax.psum_scatter(scaled.astype(jnp.bfloat16), 'ctx', scatter_dimension=1,...  25.6 us
    unnamed x4, waiting for transfers between devices  21.8 us
    ppermute x3, waiting for transfers between devices, body(): part = lax.ppermute(part, 'head', [(d, d ^ mask) for d in range(ways)])  16.6 us
    all_to_all x1, blocking collectives, body(): lax.all_to_all(packed.astype(jnp.bfloat16), 'head', split_axis=1, concat_...  13.1 us
    dot_general x4, matrix products, attend(): jnp.einsum('hqk,khd->hqd', weights.astype(jnp.bfloat16), value_rows, pref...  10.4 us
    pmax x1, blocking collectives, body(): overall = lax.pmax(maxima, 'ctx')  10.3 us
    another operation x1, loops' own time, body(): maxima, totals, partials = lax.map(attend, jnp.arange(block_count))  7.68 us
    reduce_sum x4, other arithmetic, attend(): row_total = jnp.sum(weights, axis=2)  7.21 us
  transfers between devices with their start and end apart: 6, of which 4 were waited for; matrix products, arithmetic and copies ran while one was open for 6% of the time, Pallas kernels for 0%

profile of v1, /device:TPU:0, one launch (start us, length us, event | category | flops | bytes accessed | tf_op | source)
XLA Modules:
  0.0 178.9 jit_solution(2697159791538923040)
XLA Ops:
  8.4 3.4 %convolution_convert_fusion = bf16[256,2048]{1,0:T(8,128)(2,1)S(1)} fusion(bf16[256,1024]{1,0:T(8,128)(2,1)S(1)} %copy-done, bf16[1024,2048]{1,0:T(8,128)(2,1)} %param.8), kind=kOutput, calls=%fused_computation.14 | convolution fusion | flops 1074266112 | bytes 5767168 | tf_op jit(solution)/shard_map/dot_general | solution.py:17
  12.4 1.1 broadcast_in_dim.23
  14.3 3.0 %collective-permute-start = (bf16[256,4,128]{0,2,1:T(8,128)(2,1)S(1)}, bf16[256,4,128]{0,2,1:T(8,128)(2,1)S(1)}, u32[]{:S(2)}, u32[]{:S(2)}) collective-permute-start(bf16[256,4,128]{0,2,1:T(8,128)(2,1)S(1)} %get-tuple-element.94), channel_id=1, source_target_pairs={{0,1},{1,0},{2,3},{3,2},{4,5},{5,4},{6,7},{7,6},{8,9},{9,8},{10,11... | collective-permute-start | bytes 786440 | tf_op jit(solution)/shard_map/ppermute | solution.py:29
  17.4 2.6 %collective-permute-start.1 = (bf16[256,4,128]{0,2,1:T(8,128)(2,1)S(1)}, bf16[256,4,128]{0,2,1:T(8,128)(2,1)S(1)}, u32[]{:S(2)}, u32[]{:S(2)}) collective-permute-start(bf16[256,4,128]{0,2,1:T(8,128)(2,1)S(1)} %get-tuple-element.93), channel_id=1, source_target_pairs={{0,2},{1,3},{2,0},{3,1},{4,6},{5,7},{6,4},{7,5},{8,10},{9,11},{10,... | collective-permute-start | bytes 786440 | tf_op jit(solution)/shard_map/ppermute | solution.py:29
  20.0 1.3 copy.31
  21.3 7.2 %collective-permute-done = bf16[256,4,128]{0,2,1:T(8,128)(2,1)S(1)} collective-permute-done((bf16[256,4,128]{0,2,1:T(8,128)(2,1)S(1)}, bf16[256,4,128]{0,2,1:T(8,128)(2,1)S(1)}, u32[]{:S(2)}, u32[]{:S(2)}) %collective-permute-start) | collective-permute-done | bytes 262176 | tf_op jit(solution)/shard_map/ppermute | solution.py:29
  29.3 9.4 %collective-permute-done.1 = bf16[256,4,128]{0,2,1:T(8,128)(2,1)S(1)} collective-permute-done((bf16[256,4,128]{0,2,1:T(8,128)(2,1)S(1)}, bf16[256,4,128]{0,2,1:T(8,128)(2,1)S(1)}, u32[]{:S(2)}, u32[]{:S(2)}) %collective-permute-start.1) | collective-permute-done | bytes 262176 | tf_op jit(solution)/shard_map/ppermute | solution.py:29
  40.2 1.3 fusion.17
  41.5 33.5 %while.14 = (s32[]{:T(128)}, f32[4,4,512]{2,1,0:T(4,128)S(1)}, f32[4,4,512]{2,1,0:T(4,128)S(1)}, f32[4,4,512,64]{2,3,1,0:T(8,128)}, s32[4]{0:T(128)S(1)}, /*inde...) while((s32[]{:T(128)}, f32[4,4,512]{2,1,0:T(4,128)S(1)}, ...), condition=%wide.region_3.4_spmd, body=%wide.region_0.3_spmd.sunk | while | flops 553644032 | bytes 27067044 | solution.py:54
  44.1 1.4 multiply_reduce_fusion.3
  45.4 2.6 %fusion.33 = f32[4,4,512,64]{2,3,1,0:T(8,128)} fusion(f32[4,4,512,64]{2,3,1,0:T(8,128)} %get-tuple-element.167, s32[]{:T(128)} %get-tuple-element.164, bf16[1024,4,64]{0,2,1:T(8,128)(2,1)S(1)} %get-tuple-element.182, f32[4,512,1024]{2,1,0:T(8,128)S(1)} %get-tuple-element.149, f32[4,512]{1,0:T(4,128)S(1)} %get-tuple-element.150), kind=kOutput, calls=%fused_computation.6.clone.1 | convolution fusion | flops 274726912 | bytes 9445888 | tf_op jit(solution)/shard_map/while/body/eval_jaxpr/hqk,khd->hqd/dot_general | solution.py:46
  48.0 1.8 %fusion.32 = f32[4,512]{1,0:T(4,128)S(1)} fusion(f32[4,512,1024]{2,1,0:T(8,128)S(1)} %get-tuple-element.149, f32[4,512]{1,0:T(4,128)S(1)} %get-tuple-element.150), kind=kLoop, calls=%fused_computation.3.clone.1 | loop fusion | flops 6289408 | bytes 8404992 | tf_op jit(solution)/shard_map/while/body/eval_jaxpr/reduce_sum | solution.py:45
  52.4 1.4 multiply_reduce_fusion.3
  53.8 2.6 %fusion.33 = f32[4,4,512,64]{2,3,1,0:T(8,128)} fusion(f32[4,4,512,64]{2,3,1,0:T(8,128)} %get-tuple-element.167, s32[]{:T(128)} %get-tuple-element.164, bf16[1024,4,64]{0,2,1:T(8,128)(2,1)S(1)} %get-tuple-element.182, f32[4,512,1024]{2,1,0:T(8,128)S(1)} %get-tuple-element.149, f32[4,512]{1,0:T(4,128)S(1)} %get-tuple-element.150), kind=kOutput, calls=%fused_computation.6.clone.1 | convolution fusion | flops 274726912 | bytes 9445888 | tf_op jit(solution)/shard_map/while/body/eval_jaxpr/hqk,khd->hqd/dot_general | solution.py:46
  56.4 1.8 %fusion.32 = f32[4,512]{1,0:T(4,128)S(1)} fusion(f32[4,512,1024]{2,1,0:T(8,128)S(1)} %get-tuple-element.149, f32[4,512]{1,0:T(4,128)S(1)} %get-tuple-element.150), kind=kLoop, calls=%fused_computation.3.clone.1 | loop fusion | flops 6289408 | bytes 8404992 | tf_op jit(solution)/shard_map/while/body/eval_jaxpr/reduce_sum | solution.py:45
  60.8 1.4 multiply_reduce_fusion.3
  62.2 2.6 %fusion.33 = f32[4,4,512,64]{2,3,1,0:T(8,128)} fusion(f32[4,4,512,64]{2,3,1,0:T(8,128)} %get-tuple-element.167, s32[]{:T(128)} %get-tuple-element.164, bf16[1024,4,64]{0,2,1:T(8,128)(2,1)S(1)} %get-tuple-element.182, f32[4,512,1024]{2,1,0:T(8,128)S(1)} %get-tuple-element.149, f32[4,512]{1,0:T(4,128)S(1)} %get-tuple-element.150), kind=kOutput, calls=%fused_computation.6.clone.1 | convolution fusion | flops 274726912 | bytes 9445888 | tf_op jit(solution)/shard_map/while/body/eval_jaxpr/hqk,khd->hqd/dot_general | solution.py:46
  64.8 1.8 %fusion.32 = f32[4,512]{1,0:T(4,128)S(1)} fusion(f32[4,512,1024]{2,1,0:T(8,128)S(1)} %get-tuple-element.149, f32[4,512]{1,0:T(4,128)S(1)} %get-tuple-element.150), kind=kLoop, calls=%fused_computation.3.clone.1 | loop fusion | flops 6289408 | bytes 8404992 | tf_op jit(solution)/shard_map/while/body/eval_jaxpr/reduce_sum | solution.py:45
  69.2 1.4 multiply_reduce_fusion.3
  70.6 2.6 %fusion.33 = f32[4,4,512,64]{2,3,1,0:T(8,128)} fusion(f32[4,4,512,64]{2,3,1,0:T(8,128)} %get-tuple-element.167, s32[]{:T(128)} %get-tuple-element.164, bf16[1024,4,64]{0,2,1:T(8,128)(2,1)S(1)} %get-tuple-element.182, f32[4,512,1024]{2,1,0:T(8,128)S(1)} %get-tuple-element.149, f32[4,512]{1,0:T(4,128)S(1)} %get-tuple-element.150), kind=kOutput, calls=%fused_computation.6.clone.1 | convolution fusion | flops 274726912 | bytes 9445888 | tf_op jit(solution)/shard_map/while/body/eval_jaxpr/hqk,khd->hqd/dot_general | solution.py:46
  73.2 1.8 %fusion.32 = f32[4,512]{1,0:T(4,128)S(1)} fusion(f32[4,512,1024]{2,1,0:T(8,128)S(1)} %get-tuple-element.149, f32[4,512]{1,0:T(4,128)S(1)} %get-tuple-element.150), kind=kLoop, calls=%fused_computation.3.clone.1 | loop fusion | flops 6289408 | bytes 8404992 | tf_op jit(solution)/shard_map/while/body/eval_jaxpr/reduce_sum | solution.py:45
  75.0 10.3 %pmax.7 = f32[4,2048]{1,0:T(4,128)S(1)} all-reduce(f32[4,2048]{1,0:T(4,128)S(1)} %bitcast.70), channel_id=1, replica_groups=mesh['groups'=2,'ctx'=4,'head'=4] {'ctx'}, use_global_device_ids=true, to_apply=%region_4.5 | all-reduce | flops 8192 | bytes 65536 | tf_op jit(solution)/shard_map/pmax | solution.py:59
  85.3 2.6 %mul.69 = f32[4,2048,64]{2,1,0:T(8,128)} broadcast(f32[4,2048]{1,0:T(4,128)S(1)} %get-tuple-element.85), dimensions={0,1} | broadcast | bytes 2129920 | tf_op jit(solution)/shard_map/mul | solution.py:61
  87.9 3.3 %mul.70 = f32[4,1024,128]{2,1,0:T(8,128)S(1)} reshape(f32[4,2048,64]{2,1,0:T(8,128)} %mul.69) | data formatting | bytes 4194304 | tf_op jit(solution)/shard_map/mul | solution.py:61
  91.1 3.8 %copy.23 = f32[4,4,512,64]{3,2,1,0:T(8,128)} copy(f32[4,4,512,64]{2,3,0,1:T(8,128)} %bitcast.66) | data formatting | bytes 4194304 | tf_op jit(solution)/shard_map/transpose | solution.py:57
  94.9 4.6 %reshape_reshape.3 = f32[4,1024,128]{2,1,0:T(8,128)} reshape(f32[4,4,512,64]{3,2,1,0:T(8,128)} %copy.23) | data formatting | bytes 4194304 | tf_op jit(solution)/shard_map/reshape;reshape | solution.py:61
  100.7 2.8 %multiply_convert_fusion = bf16[4,1024,128]{2,1,0:T(8,128)(2,1)} fusion(f32[4,1024,128]{2,1,0:T(8,128)} %reshape_reshape.3, f32[4,1024,128]{2,1,0:T(8,128)S(1)} %mul.70), kind=kLoop, calls=%fused_computation.15 | loop fusion | flops 1048576 | bytes 5242880 | tf_op jit(solution)/shard_map/convert_element_type | solution.py:65
  104.1 21.2 %reduce-scatter.7.cloned.1.call-done = bf16[512,4]{1,0:T(8,128)(2,1)} async-done(((bf16[2048,4]{1,0:T(8,128)(2,1)}), bf16[512,4]{1,0:T(8,128)(2,1)}) %reduce-scatter.7.cloned.1.call-update) | async-done | bytes 4112
  127.1 25.6 %reduce-scatter.5.cloned.1.call-done = bf16[4,256,128]{2,1,0:T(8,128)(2,1)} async-done(((bf16[4,1024,128]{2,1,0:T(8,128)(2,1)}), bf16[4,256,128]{2,1,0:T(8,128)(2,1)}) %reduce-scatter.5.cloned.1.call-update) | async-done | bytes 262160 | tf_op jit(solution)/shard_map/reduce_scatter | solution.py:64
  152.7 1.2 reshape.56
  154.2 13.1 %all_to_all.4 = bf16[4,4,8192]{2,0,1:T(4,128)(2,1)S(1)} all-to-all(bf16[4,4,8192]{2,0,1:T(4,128)(2,1)S(1)} %copy.24), channel_id=1, replica_groups=mesh['groups'=2,'ctx'=4,'head'=4] {'head'}, dimensions={1} | all-to-all | bytes 524288 | tf_op jit(solution)/shard_map/all_to_all | solution.py:75
  168.7 2.8 %convolution_convert_fusion.1 = bf16[128,1024]{1,0:T(8,128)(2,1)} fusion(bf16[128,1024]{0,1:T(8,128)(2,1)S(1)} %fusion.16, bf16[1024,1024]{1,0:T(8,128)(2,1)} %all-gather.2.cloned.1.call-done), kind=kOutput, calls=%fused_computation.16 | convolution fusion | flops 268566528 | bytes 2621440 | tf_op jit(solution)/shard_map/dot_general | solution.py:85
  (43 shorter events, 12.4 us)
Async XLA Ops:
  7.4 1.0 copy-start
  7.4 117.9 %reduce-scatter.7.cloned.1.call-start = ((), (), s32[]{:S(2)}) async-start(), calls=%async_computation.5 | async-start | bytes 655360
  14.3 14.2 %collective-permute-start = (bf16[256,4,128]{0,2,1:T(8,128)(2,1)S(1)}, bf16[256,4,128]{0,2,1:T(8,128)(2,1)S(1)}, u32[]{:S(2)}, u32[]{:S(2)}) collective-permute-start(bf16[256,4,128]{0,2,1:T(8,128)(2,1)S(1)} %get-tuple-element.94), channel_id=1, source_target_pairs={{0,1},{1,0},{2,3},{3,2},{4,5},{5,4},{6,7},{7,6},{8,9},{9,8},{10,11... | collective-permute-start | bytes 786440 | tf_op jit(solution)/shard_map/ppermute | solution.py:29
  17.4 21.3 %collective-permute-start.1 = (bf16[256,4,128]{0,2,1:T(8,128)(2,1)S(1)}, bf16[256,4,128]{0,2,1:T(8,128)(2,1)S(1)}, u32[]{:S(2)}, u32[]{:S(2)}) collective-permute-start(bf16[256,4,128]{0,2,1:T(8,128)(2,1)S(1)} %get-tuple-element.93), channel_id=1, source_target_pairs={{0,2},{1,3},{2,0},{3,1},{4,6},{5,7},{6,4},{7,5},{8,10},{9,11},{10,... | collective-permute-start | bytes 786440 | tf_op jit(solution)/shard_map/ppermute | solution.py:29
  20.0 19.5 %collective-permute-start.2 = (bf16[256,4,128]{0,2,1:T(8,128)(2,1)S(1)}, bf16[256,4,128]{0,2,1:T(8,128)(2,1)S(1)}, u32[]{:S(2)}, u32[]{:S(2)}) collective-permute-start(bf16[256,4,128]{0,2,1:T(8,128)(2,1)S(1)} %get-tuple-element.92), channel_id=1, source_target_pairs={{0,3},{1,2},{2,1},{3,0},{4,7},{5,6},{6,5},{7,4},{8,11},{9,10},{10,... | collective-permute-start | bytes 786440 | tf_op jit(solution)/shard_map/ppermute | solution.py:29
  100.6 52.0 %reduce-scatter.5.cloned.1.call-start = ((), (), s32[]{:S(2)}) async-start(), calls=%async_computation.3 | async-start | bytes 1310720 | tf_op jit(solution)/shard_map/reduce_scatter | solution.py:64
  103.5 65.2 %all-gather.2.cloned.1.call-start = ((), (), s32[]{:S(2)}) async-start(), calls=%async_computation.4 | async-start | bytes 2621440 | tf_op jit(solution)/shard_map/all_gather | solution.py:87
  127.1 41.3 %copy-start.1 = (f32[1024]{0:T(1024)S(1)}, f32[1024]{0:T(1024)}, u32[]{:S(2)}) copy-start(f32[1024]{0:T(1024)} %param.10) | copy-start | bytes 12292
Sparse Core Ops, SparseCore 0:
  100.7 24.5 reduce-scatter.6
  127.8 24.7 reduce-scatter.4
Sparse Core Ops, SparseCore 1:
  105.5 48.4 all-gather.1
